TPU v7x, 32 devices: a whole 2x2x4 slice. The times are simulated.
32 devices in a mesh: var: 4 (over x, core), space: 8 (over z, y).
Axes of the slice: x: 2, y: 2, z: 4, core: 2. Of those that a mesh axis runs over, the one named last changes fastest.
Arguments:
- fields: bfloat16 [8, 1024, 32768], P('var', None, 'space'), may hold values from -6 to 6
- eigenfunctions: bfloat16 [8, 64, 32768], P('var', None, 'space'), may hold values from -0.03125 to 0.03125
- start: float32 [512, 128], replicated, may hold values from -6 to 6
- grid_count: int32 [8], replicated, may hold values from 16384 to 32768
Outputs:
- loadings: bfloat16 [8, 128, 32768], P('var', None, 'space')
- component_scores: float32 [1024, 128], replicated
- explained: float32 [8, 1024], P('var')
Inputs may be any that keep to these rules, and one draw needn't show every extreme that they name: The grid of variable v is its points 0 to grid_count[v] - 1.
All inputs are finite; a program needn't handle non-finite values.
Results may differ from a plain program's by a relative error of at most 0.005.
Values sent between devices are 32-bit elements; how exact they have to be, the bound alone decides.
A program may use at most 64 MiB of HBM per device.

v0:
```python
import jax
import jax.numpy as jnp
from jax import lax
from jax.sharding import PartitionSpec as P

M = 64
SWEEPS = 2


def orthogonalize(image, gram):
    lower = jnp.linalg.cholesky(gram)
    return jax.scipy.linalg.solve_triangular(lower, image.T, lower=True).T


def product(left, right):
    return jnp.dot(left, right, precision=lax.Precision.HIGHEST, preferred_element_type=jnp.float32)


def shards(fields, eigenfunctions, start, grid_count):
    local_vars, samples, local_points = fields.shape
    first_var = lax.axis_index("var") * local_vars
    counts = lax.dynamic_slice_in_dim(grid_count, first_var, local_vars, 0)
    points = lax.axis_index("space") * local_points + jnp.arange(local_points, dtype=jnp.int32)
    valid = points[None, :] < counts[:, None]
    masked = jnp.where(valid[:, None, :], eigenfunctions, jnp.zeros((), eigenfunctions.dtype))
    part = jnp.einsum("vng,vmg->nvm", fields, masked, preferred_element_type=jnp.float32)
    summed = lax.psum(part.reshape(samples, local_vars * M), "space")
    joint = lax.all_gather(summed, "var", axis=1, tiled=True)
    centred = joint - jnp.mean(joint, axis=0, keepdims=True)
    basis = start
    cov = product(centred.T, centred) / (samples - 1)
    for sweep in range(SWEEPS):
        image = product(cov, basis)
        basis = orthogonalize(image, product(image.T, image))
    component_scores = product(centred, basis)
    scores_low = component_scores.astype(jnp.bfloat16)
    own_basis = lax.dynamic_slice_in_dim(basis, first_var * M, local_vars * M, 0)
    basis_low = own_basis.astype(jnp.bfloat16).reshape(local_vars, M, basis.shape[1])
    loadings = jnp.einsum(
        "vmk,vmg->vkg", basis_low, masked, preferred_element_type=jnp.float32
    ).astype(jnp.bfloat16)
    partial_gain = []
    for local in range(local_vars):
        rebuilt = jnp.dot(scores_low, loadings[local], preferred_element_type=jnp.float32)
        wide = fields[local].astype(jnp.float32)
        deviation = wide - jnp.mean(wide, axis=0, keepdims=True)
        partial_gain.append(jnp.sum(2.0 * deviation * rebuilt - rebuilt * rebuilt, axis=1) / M)
    explained = lax.psum(jnp.stack(partial_gain, axis=0), "space")
    return (loadings, component_scores, explained)


def solution(mesh):
    return jax.shard_map(
        shards,
        mesh=mesh,
        in_specs=(P("var", None, "space"), P("var", None, "space"), P(), P()),
        out_specs=(P("var", None, "space"), P(), P("var", None)),
        check_vma=False,
    )
```

profile of v0, /device:TPU:0, one launch (start us, length us, event | category | flops | bytes accessed | tf_op | source)
XLA Modules:
  0.0 234.2 jit_solution(11181255422536817181)
XLA Ops:
  7.2 0.0 copy-start
  7.2 0.0 all-reduce.2.cloned.1.call-start
  7.2 0.7 dynamic_slice.6
  8.0 0.1 broadcast_compare_fusion
  8.1 12.1 %fusion.19 = f32[2,64,1024]{2,1,0:T(8,128)} fusion(bf16[2,1024,4096]{2,1,0:T(8,128)(2,1)} %param.7, bf16[2,64,4096]{2,1,0:T(8,128)(2,1)} %param.8, pred[2,4096]{1,0:T(4,128)(4,1)S(1)} %broadcast_compare_fusion), kind=kOutput, calls=%fused_computation.25 | convolution fusion | flops 1074266112 | bytes 18358272 | tf_op jit(solution)/shard_map/vng,vmg->nvm/dot_general | solution.py:26
  20.2 0.0 all-reduce.2.cloned.1.call-update
  20.2 0.0 all-gather.2.cloned.1.call-start
  20.2 75.6 %all-reduce.2.cloned.1.call-done = f32[1024,128]{0,1:T(8,128)} async-done(((f32[1024,128]{0,1:T(8,128)}), f32[1024,128]{0,1:T(8,128)}) %all-reduce.2.cloned.1.call-update) | async-done | bytes 524304 | tf_op jit(solution)/shard_map/psum | solution.py:27
  95.8 0.0 all-gather.2.cloned.1.call-update
  95.9 7.8 %convert_reduce_fusion.1 = (f32[4096]{0:T(1024)S(1)}, f32[4096]{0:T(1024)S(1)}) fusion(bf16[2,1024,4096]{2,1,0:T(8,128)(2,1)} %param.7), kind=kLoop, calls=%fused_computation.2 | loop fusion | flops 16769024 | bytes 16809984 | tf_op jit(solution)/shard_map/reduce_sum | solution.py:46
  103.6 0.6 broadcast_multiply_fusion
  104.2 14.9 %all-gather.2.cloned.1.call-done = f32[1024,512]{0,1:T(8,128)} async-done(((f32[1024,128]{0,1:T(8,128)}), f32[1024,512]{0,1:T(8,128)}) %all-gather.2.cloned.1.call-update) | async-done | bytes 2097168 | tf_op jit(solution)/shard_map/all_gather | solution.py:28
  119.2 1.9 reduce_sum.45
  121.1 0.0 copy-start.10
  121.1 5.9 %fusion.14 = f32[512,512]{1,0:T(8,128)S(1)} fusion(f32[1024,512]{0,1:T(8,128)} %all-gather.2.cloned.1.call-done, f32[512]{0:T(512)S(1)} %broadcast_multiply_fusion.4), kind=kOutput, calls=%fused_computation.19 | convolution fusion | flops 3222011904 | bytes 3147776 | tf_op jit(solution)/shard_map/dot_general | solution.py:16
  127.0 0.0 copy-done.10
  127.0 0.0 copy-start.3
  127.0 1.0 copy-done.3
  128.0 0.0 copy-done
  128.0 1.0 fusion.39
  129.0 0.0 copy-start.5
  129.0 0.7 copy-done.5
  129.7 0.6 fusion.40
  130.3 0.1 copy.10
  130.4 0.6 fusion.33
  131.0 12.5 %cholesky.44 = f32[128,128]{1,0:T(8,128)S(1)} custom-call(f32[128,128]{1,0:T(8,128)} %fusion.33), custom_call_target="Cholesky" | custom-call | tf_op jit(solution)/shard_map/jit(cholesky)/cholesky | solution.py:11
  143.6 0.6 compare_reduce_fusion.1
  144.3 0.6 fusion.28
  144.9 9.8 %custom-call.6 = f32[1,128,128]{1,2,0:T(8,128)S(1)} custom-call(f32[1,128,128]{2,1,0:T(8,128)S(1)} %fusion.28), custom_call_target="InvertDiagBlocksLowerTriangular" | custom-call | tf_op jit(solution)/shard_map/jit(_solve_triangular)/triangular_solve | solution.py:12
  154.7 1.4 fusion.24
  156.1 2.5 %fusion.41 = f32[512,128]{1,0:T(8,128)S(1)} fusion(f32[512,512]{1,0:T(8,128)} %copy-done.3, f32[128,512]{1,0:T(8,128)S(1)} %fusion.24), kind=kOutput, calls=%fused_computation.65 | convolution fusion | flops 402653184 | bytes 1572864 | tf_op jit(solution)/shard_map/dot_general | solution.py:16
  158.6 0.0 copy-start.4
  158.6 0.7 copy-done.4
  159.3 0.6 fusion.42
  159.9 0.1 copy.11
  160.0 0.6 fusion.31
  160.6 12.5 %cholesky.55 = f32[128,128]{1,0:T(8,128)S(1)} custom-call(f32[128,128]{1,0:T(8,128)} %fusion.31), custom_call_target="Cholesky" | custom-call | tf_op jit(solution)/shard_map/jit(cholesky)/cholesky | solution.py:11
  173.2 0.6 compare_reduce_fusion
  173.8 0.7 fusion.29
  174.5 9.8 %custom-call.7 = f32[1,128,128]{1,2,0:T(8,128)S(1)} custom-call(f32[1,128,128]{2,1,0:T(8,128)S(1)} %fusion.29), custom_call_target="InvertDiagBlocksLowerTriangular" | custom-call | tf_op jit(solution)/shard_map/jit(_solve_triangular)/triangular_solve | solution.py:12
  184.3 1.4 fusion.22
  185.7 0.0 copy-start.7
  185.7 0.7 copy-done.7
  186.4 0.1 copy.12
  186.5 0.0 copy-done.1
  186.5 0.8 convolution_convert_fusion
  187.3 0.0 copy-done.2
  187.3 0.0 copy-start.6
  187.3 4.7 %fusion.10 = f32[1024,128]{1,0:T(8,128)S(1)} fusion(f32[128,512]{1,0:T(8,128)} %copy-done.7, f32[1024,512]{0,1:T(8,128)S(1)} %copy-done.2, f32[512]{0:T(512)} %copy-done.10), kind=kOutput, calls=%fused_computation.15 | convolution fusion | flops 805830656 | bytes 2885632 | tf_op jit(solution)/shard_map/dot_general | solution.py:16
  192.0 0.0 copy-start.8
  192.0 0.0 slice-start
  192.0 0.0 copy-start.9
  192.0 0.0 slice-start.1
  192.1 0.0 slice-start.2
  192.1 0.0 slice-start.3
  192.1 7.2 %fusion.9 = f32[1024]{0:T(1024)S(1)} fusion(f32[4096]{0:T(1024)} %get-tuple-element.7, bf16[2,1024,4096]{2,1,0:T(8,128)(2,1)} %param.7, bf16[2,128,4096]{2,1,0:T(8,128)(2,1)S(1)} %convolution_convert_fusion, f32[1024,128]{1,0:T(8,128)S(1)} %fusion.10), kind=kOutput, calls=%fused_computation.13 | convolution fusion | flops 1103232000 | bytes 9981952 | tf_op jit(solution)/shard_map/dot_general | solution.py:44
  199.3 0.0 copy-done.6
  199.3 0.0 slice-done
  199.3 0.0 copy-done.9
  199.3 0.0 slice-done.1
  199.3 0.0 slice-done.2
  199.4 1.2 slice-done.3
  200.5 4.5 %fusion.4 = f32[1024]{0:T(1024)S(1)} fusion(f32[4096]{0:T(1024)S(1)} %copy-done.9, bf16[2,1024,4096]{2,1,0:T(8,128)(2,1)S(1)} %bitcast.74, bf16[2,128,4096]{2,1,0:T(8,128)(2,1)S(1)} %convolution_convert_fusion, f32[1024,128]{1,0:T(8,128)S(1)} %fusion.10), kind=kOutput, calls=%fused_computation.8 | convolution fusion | flops 1103232000 | bytes 9981952 | tf_op jit(solution)/shard_map/dot_general | solution.py:44
  205.2 22.2 %psum.15 = f32[2,1024]{1,0:T(2,128)} all-reduce(f32[2,1024]{1,0:T(2,128)S(1)} %pad_maximum_fusion), channel_id=1, replica_groups=mesh['var'=4,'space'=8] {'space'}, use_global_device_ids=true, to_apply=%region_8.11 | all-reduce | flops 2048 | bytes 16384 | tf_op jit(solution)/shard_map/psum | solution.py:48
  (12 shorter events, 0.1 us)
Async XLA Ops:
  7.2 120.8 %copy-start = (f32[512,128]{1,0:T(8,128)S(1)}, f32[512,128]{1,0:T(8,128)}, u32[]{:S(2)}) copy-start(f32[512,128]{1,0:T(8,128)} %param.9) | copy-start | bytes 786436
  7.2 88.6 %all-reduce.2.cloned.1.call-start = ((), (), s32[]{:S(2)}) async-start(), calls=%async_computation | async-start | bytes 1048576 | tf_op jit(solution)/shard_map/psum | solution.py:27
  20.2 166.4 %copy-start.1 = (bf16[2,64,4096]{2,1,0:T(8,128)(2,1)S(1)}, bf16[2,64,4096]{2,1,0:T(8,128)(2,1)}, u32[]{:S(2)}) copy-start(bf16[2,64,4096]{2,1,0:T(8,128)(2,1)} %param.8) | copy-start | bytes 3145732
  20.2 99.0 %all-gather.2.cloned.1.call-start = ((), (), s32[]{:S(2)}) async-start(), calls=%async_computation.1 | async-start | bytes 2621440 | tf_op jit(solution)/shard_map/all_gather | solution.py:28
  119.2 68.1 %copy-start.2 = (f32[1024,512]{0,1:T(8,128)S(1)}, f32[1024,512]{0,1:T(8,128)}, u32[]{:S(2)}) copy-start(f32[1024,512]{0,1:T(8,128)} %all-gather.2.cloned.1.call-done) | copy-start | bytes 6291460
  121.1 5.9 %copy-start.10 = (f32[512]{0:T(512)}, f32[512]{0:T(512)S(1)}, u32[]{:S(2)}) copy-start(f32[512]{0:T(512)S(1)} %broadcast_multiply_fusion.4) | copy-start | bytes 6148
  127.0 1.0 copy-start.3
  129.0 0.7 copy-start.5
  158.6 0.7 copy-start.4
  185.7 0.7 copy-start.7
  187.3 12.0 %copy-start.6 = (bf16[2,128,4096]{2,1,0:T(8,128)(2,1)}, bf16[2,128,4096]{2,1,0:T(8,128)(2,1)S(1)}, u32[]{:S(2)}) copy-start(bf16[2,128,4096]{2,1,0:T(8,128)(2,1)S(1)} %convolution_convert_fusion) | copy-start | bytes 6291460
  192.0 13.1 %copy-start.8 = (f32[1024,128]{1,0:T(8,128)}, f32[1024,128]{1,0:T(8,128)S(1)}, u32[]{:S(2)}) copy-start(f32[1024,128]{1,0:T(8,128)S(1)} %fusion.10) | copy-start | bytes 1572868
  192.0 7.3 %slice-start = ((s8[16777216]{0:T(1024)(128)(4,1)}), s8[4194304]{0:T(1024)(128)(4,1)S(1)}, s32[]{:S(2)}) async-start(s8[16777216]{0:T(1024)(128)(4,1)} %bitcast.73), calls=%async_computation.2 | async-start | bytes 8388608
  192.0 7.3 %copy-start.9 = (f32[4096]{0:T(1024)S(1)}, f32[4096]{0:T(1024)}, u32[]{:S(2)}) copy-start(f32[4096]{0:T(1024)} %get-tuple-element.8) | copy-start | bytes 49156
  192.0 7.3 %slice-start.1 = ((s8[16777216]{0:T(1024)(128)(4,1)}), s8[4194304]{0:T(1024)(128)(4,1)S(1)}, s32[]{:S(2)}) async-start(s8[16777216]{0:T(1024)(128)(4,1)} %bitcast.73), calls=%async_computation.3 | async-start | bytes 8388608
  192.1 7.3 %slice-start.2 = ((s8[16777216]{0:T(1024)(128)(4,1)}), s8[4194304]{0:T(1024)(128)(4,1)S(1)}, s32[]{:S(2)}) async-start(s8[16777216]{0:T(1024)(128)(4,1)} %bitcast.73), calls=%async_computation.4 | async-start | bytes 8388608
  192.1 8.5 %slice-start.3 = ((s8[16777216]{0:T(1024)(128)(4,1)}), s8[4194304]{0:T(1024)(128)(4,1)S(1)}, s32[]{:S(2)}) async-start(s8[16777216]{0:T(1024)(128)(4,1)} %bitcast.73), calls=%async_computation.5 | async-start | bytes 8388608
Sparse Core Ops, SparseCore 0:
  20.3 75.4 all-reduce.1
  97.4 21.7 all-gather.1
where the time goes:
time: 235 us; the launch traced here: 234 us
  waiting for transfers between devices  90.5 us (39%)
  other arithmetic  59 us (25%)
  matrix products  42.6 us (18%)
  blocking collectives  22.2 us (9%)
  between operations  14.4 us (6%)
  local copies, waits for them, and re-layouts  5.37 us (2%)
    psum x1, waiting for transfers between devices, shards(): summed = lax.psum(part.reshape(samples, local_vars * M), 'space')  75.6 us
    another operation x6, other arithmetic, orthogonalize(): lower = jnp.linalg.cholesky(gram)  26.4 us
    psum x1, blocking collectives, shards(): explained = lax.psum(jnp.stack(partial_gain, axis=0), 'space')  22.2 us
    another operation x4, other arithmetic, orthogonalize(): return jax.scipy.linalg.solve_triangular(lower, image.T, lower=True).T  20.9 us
    dot_general x6, matrix products, product(): jnp.dot(left, right, precision=lax.Precision.HIGHEST, preferred_element_t...  15.2 us
    all_gather x1, waiting for transfers between devices, shards(): joint = lax.all_gather(summed, 'var', axis=1, tiled=True)  14.9 us
    dot_general x1, matrix products, shards(): jnp.einsum('vng,vmg->nvm', fields, masked, preferred_element_type=jnp.flo...  12.1 us
    dot_general x2, matrix products, shards(): jnp.dot(scores_low, loadings[local], preferred_element_type=jnp.float32)  11.8 us
  transfers between devices with their start and end apart: 2, of which 2 were waited for; matrix products, arithmetic and copies ran while one was open for 4% of the time, Pallas kernels for 0%

commit v1 on v0

--- a/solution.py
+++ b/solution.py
@@ -25,7 +25,12 @@
     masked = jnp.where(valid[:, None, :], eigenfunctions, jnp.zeros((), eigenfunctions.dtype))
     part = jnp.einsum("vng,vmg->nvm", fields, masked, preferred_element_type=jnp.float32)
     summed = lax.psum(part.reshape(samples, local_vars * M), "space")
-    joint = lax.all_gather(summed, "var", axis=1, tiled=True)
+    ring = [summed]
+    for hop in range(3):
+        ring.append(lax.ppermute(ring[-1], "var", [(dev, (dev + 1) % 4) for dev in range(4)]))
+    joint = jnp.roll(
+        jnp.concatenate(ring[::-1], axis=1), (lax.axis_index("var") + 1) * ring[0].shape[1], axis=1
+    )
     centred = joint - jnp.mean(joint, axis=0, keepdims=True)
     basis = start
     cov = product(centred.T, centred) / (samples - 1)

time: 235 us -> 223 us (0.949)
  other arithmetic: 59 us -> 53.8 us
  matrix products: 42.6 us -> 38.6 us
  local copies, waits for them, and re-layouts: 5.37 us -> 1.48 us
  waiting for transfers between devices: 90.5 us -> 93.8 us
    ppermute x0 -> x3, waiting for transfers between devices: none -> 18.2 us  [shards(): lax.ppermute(ring[-1], 'var', [(dev, (dev + 1) % 4) for dev in range(4)])]
    all_gather x1 -> x0, waiting for transfers between devices: 14.9 us -> none  [shards(): joint = lax.all_gather(summed, 'var', axis=1, tiled=True)]
    unnamed x30 -> x27, local copies, waits for them, and re-layouts: 4.33 us -> 0.4 us
    dot_general x6, matrix products: 15.2 us -> 12.2 us  [product(): jnp.dot(left, right, precision=lax.Precision.HIGHEST, preferred_element_t...]
  transfers between devices with their start and end apart: 2 -> 4, of which waited for: 2 -> 4; matrix products, arithmetic and copies ran while one was open for 4% -> 3% of each run, Pallas kernels for 0% -> 0%
where the time goes in v1:
time: 223 us
  waiting for transfers between devices  93.8 us (42%)
  other arithmetic  53.8 us (24%)
  matrix products  38.6 us (17%)
  blocking collectives  20.5 us (9%)
  between operations  14.5 us (7%)
    psum x1, waiting for transfers between devices, shards(): summed = lax.psum(part.reshape(samples, local_vars * M), 'space')  75.6 us
    another operation x6, other arithmetic, orthogonalize(): lower = jnp.linalg.cholesky(gram)  24.8 us
    another operation x4, other arithmetic, orthogonalize(): return jax.scipy.linalg.solve_triangular(lower, image.T, lower=True).T  20.9 us
    psum x1, blocking collectives, shards(): explained = lax.psum(jnp.stack(partial_gain, axis=0), 'space')  20.5 us
    ppermute x3, waiting for transfers between devices, shards(): lax.ppermute(ring[-1], 'var', [(dev, (dev + 1) % 4) for dev in range(4)])  18.2 us
    dot_general x2, matrix products, shards(): jnp.dot(scores_low, loadings[local], preferred_element_type=jnp.float32)  12.7 us
    dot_general x6, matrix products, product(): jnp.dot(left, right, precision=lax.Precision.HIGHEST, preferred_element_t...  12.2 us
    dot_general x1, matrix products, shards(): jnp.einsum('vng,vmg->nvm', fields, masked, preferred_element_type=jnp.flo...  12.1 us
  transfers between devices with their start and end apart: 4, of which 4 were waited for; matrix products, arithmetic and copies ran while one was open for 3% of the time, Pallas kernels for 0%

profile of v1, /device:TPU:0, one launch (start us, length us, event | category | flops | bytes accessed | tf_op | source)
XLA Modules:
  0.0 222.6 jit_solution(18258958401412189234)
XLA Ops:
  7.2 0.0 copy-start
  7.2 0.0 all-reduce.2.cloned.1.call-start
  7.2 0.7 dynamic_slice.10
  8.0 0.1 broadcast_compare_fusion
  8.1 12.1 %fusion.21 = f32[2,64,1024]{2,1,0:T(8,128)} fusion(bf16[2,1024,4096]{2,1,0:T(8,128)(2,1)} %param.7, bf16[2,64,4096]{2,1,0:T(8,128)(2,1)} %param.8, pred[2,4096]{1,0:T(4,128)(4,1)S(1)} %broadcast_compare_fusion), kind=kOutput, calls=%fused_computation.28 | convolution fusion | flops 1074266112 | bytes 18358272 | tf_op jit(solution)/shard_map/vng,vmg->nvm/dot_general | solution.py:26
  20.2 0.0 all-reduce.2.cloned.1.call-update
  20.2 75.6 %all-reduce.2.cloned.1.call-done = f32[1024,128]{0,1:T(8,128)} async-done(((f32[1024,128]{0,1:T(8,128)}), f32[1024,128]{0,1:T(8,128)}) %all-reduce.2.cloned.1.call-update) | async-done | bytes 524304 | tf_op jit(solution)/shard_map/psum | solution.py:27
  95.8 0.0 copy-start.4
  95.8 0.0 collective-permute-start
  95.8 8.8 %collective-permute-done = f32[1024,128]{0,1:T(8,128)S(1)} collective-permute-done((f32[1024,128]{0,1:T(8,128)}, f32[1024,128]{0,1:T(8,128)S(1)}, u32[]{:S(2)}, u32[]{:S(2)}) %collective-permute-start) | collective-permute-done | bytes 524320 | tf_op jit(solution)/shard_map/ppermute | solution.py:30
  104.6 0.0 collective-permute-start.1
  104.6 8.6 %collective-permute-done.1 = f32[1024,128]{0,1:T(8,128)S(1)} collective-permute-done((f32[1024,128]{0,1:T(8,128)S(1)}, f32[1024,128]{0,1:T(8,128)S(1)}, u32[]{:S(2)}, u32[]{:S(2)}) %collective-permute-start.1) | collective-permute-done | bytes 524320 | tf_op jit(solution)/shard_map/ppermute | solution.py:30
  113.2 0.0 collective-permute-start.2
  113.2 7.8 %convert_reduce_fusion.1 = (f32[4096]{0:T(1024)S(1)}, f32[4096]{0:T(1024)S(1)}) fusion(bf16[2,1024,4096]{2,1,0:T(8,128)(2,1)} %param.7), kind=kLoop, calls=%fused_computation.2 | loop fusion | flops 16769024 | bytes 16809984 | tf_op jit(solution)/shard_map/reduce_sum | solution.py:51
  121.0 0.8 collective-permute-done.2
  122.0 0.0 copy-done.4
  122.2 0.0 copy-start.2
  122.2 0.2 dynamic-slice_reduce_fusion
  122.4 3.7 %fusion.16 = f32[512,512]{1,0:T(8,128)S(1)} fusion(f32[1024,1024]{0,1:T(8,128)S(1)} %constant_dynamic-update-slice_fusion, s32[]{:T(128)S(6)} %select_n.29, f32[512]{0:T(512)S(1)} %broadcast_multiply_fusion.4), kind=kOutput, calls=%fused_computation.22 | convolution fusion | flops 3222011904 | bytes 3147780 | tf_op jit(solution)/shard_map/dot_general | solution.py:16
  126.1 0.0 copy-done.2
  126.1 0.0 copy-done
  126.1 1.0 fusion.43
  127.1 0.0 copy-start.1
  127.1 0.6 fusion.44
  127.7 0.1 copy.10
  127.8 11.7 %cholesky.44 = f32[128,128]{1,0:T(8,128)S(1)} custom-call(f32[128,128]{1,0:T(8,128)S(1)} %fusion.35), custom_call_target="Cholesky" | custom-call | tf_op jit(solution)/shard_map/jit(cholesky)/cholesky | solution.py:11
  139.6 0.6 compare_reduce_fusion.1
  140.2 0.7 fusion.30
  140.9 9.8 %custom-call.6 = f32[1,128,128]{1,2,0:T(8,128)S(1)} custom-call(f32[1,128,128]{2,1,0:T(8,128)S(1)} %fusion.30), custom_call_target="InvertDiagBlocksLowerTriangular" | custom-call | tf_op jit(solution)/shard_map/jit(_solve_triangular)/triangular_solve | solution.py:12
  150.7 0.4 fusion.26
  151.1 1.2 fusion.45
  152.4 0.6 fusion.46
  153.0 0.1 copy.11
  153.1 11.7 %cholesky.55 = f32[128,128]{1,0:T(8,128)S(1)} custom-call(f32[128,128]{1,0:T(8,128)S(1)} %fusion.33), custom_call_target="Cholesky" | custom-call | tf_op jit(solution)/shard_map/jit(cholesky)/cholesky | solution.py:11
  164.8 0.6 compare_reduce_fusion
  165.5 0.7 fusion.31
  166.1 9.8 %custom-call.7 = f32[1,128,128]{1,2,0:T(8,128)S(1)} custom-call(f32[1,128,128]{2,1,0:T(8,128)S(1)} %fusion.31), custom_call_target="InvertDiagBlocksLowerTriangular" | custom-call | tf_op jit(solution)/shard_map/jit(_solve_triangular)/triangular_solve | solution.py:12
  175.9 0.4 fusion.24
  176.4 5.1 %fusion.10 = f32[1024,128]{1,0:T(8,128)S(1)} fusion(f32[128,512]{1,0:T(8,128)S(1)} %fusion.24, f32[1024,1024]{0,1:T(8,128)} %copy-done.2, s32[]{:T(128)S(6)} %select_n.29, f32[512]{0:T(512)S(1)} %broadcast_multiply_fusion.4), kind=kOutput, calls=%fused_computation.15 | convolution fusion | flops 805830656 | bytes 2885636 | tf_op jit(solution)/shard_map/dot_general | solution.py:16
  181.5 0.0 copy-start.5
  181.5 0.1 copy.12
  181.6 0.0 copy-done.1
  181.7 0.0 slice-start
  181.7 0.7 convolution_convert_fusion
  182.4 0.0 copy-start.3
  182.4 0.0 slice-start.1
  182.4 0.0 slice-start.2
  182.5 0.0 slice-start.3
  182.5 8.1 %fusion.4 = f32[1024]{0:T(1024)S(1)} fusion(f32[4096]{0:T(1024)S(1)} %get-tuple-element.8, bf16[2,1024,4096]{2,1,0:T(8,128)(2,1)} %param.7, bf16[2,128,4096]{2,1,0:T(8,128)(2,1)S(1)} %convolution_convert_fusion, f32[1024,128]{1,0:T(8,128)S(1)} %fusion.10), kind=kOutput, calls=%fused_computation.8 | convolution fusion | flops 1103232000 | bytes 9981952 | tf_op jit(solution)/shard_map/dot_general | solution.py:49
  190.6 0.0 copy-done.5
  190.6 0.0 copy-done.3
  190.6 0.0 slice-done
  190.7 0.0 slice-done.1
  190.7 0.0 slice-done.2
  190.7 0.1 slice-done.3
  190.8 4.5 %fusion.9 = f32[1024]{0:T(1024)S(1)} fusion(f32[4096]{0:T(1024)S(1)} %get-tuple-element.7, bf16[2,1024,4096]{2,1,0:T(8,128)(2,1)S(1)} %bitcast.74, bf16[2,128,4096]{2,1,0:T(8,128)(2,1)S(1)} %convolution_convert_fusion, f32[1024,128]{1,0:T(8,128)S(1)} %fusion.10), kind=kOutput, calls=%fused_computation.13 | convolution fusion | flops 1103232000 | bytes 9981952 | tf_op jit(solution)/shard_map/dot_general | solution.py:49
  195.3 20.5 %psum.15 = f32[2,1024]{1,0:T(2,128)} all-reduce(f32[2,1024]{1,0:T(2,128)S(1)} %pad_maximum_fusion), channel_id=1, replica_groups=mesh['var'=4,'space'=8] {'space'}, use_global_device_ids=true, to_apply=%region_8.11 | all-reduce | flops 2048 | bytes 16384 | tf_op jit(solution)/shard_map/psum | solution.py:53
  (20 shorter events, 0.4 us)
Async XLA Ops:
  7.2 119.0 %copy-start = (f32[512,128]{1,0:T(8,128)S(1)}, f32[512,128]{1,0:T(8,128)}, u32[]{:S(2)}) copy-start(f32[512,128]{1,0:T(8,128)} %param.9) | copy-start | bytes 786436
  7.2 88.6 %all-reduce.2.cloned.1.call-start = ((), (), s32[]{:S(2)}) async-start(), calls=%async_computation | async-start | bytes 1048576 | tf_op jit(solution)/shard_map/psum | solution.py:27
  95.8 26.2 %copy-start.4 = (f32[1024,128]{0,1:T(8,128)S(1)}, f32[1024,128]{0,1:T(8,128)}, u32[]{:S(2)}) copy-start(f32[1024,128]{0,1:T(8,128)} %all-reduce.2.cloned.1.call-done) | copy-start | bytes 1572868
  95.8 8.8 %collective-permute-start = (f32[1024,128]{0,1:T(8,128)}, f32[1024,128]{0,1:T(8,128)S(1)}, u32[]{:S(2)}, u32[]{:S(2)}) collective-permute-start(f32[1024,128]{0,1:T(8,128)} %all-reduce.2.cloned.1.call-done), channel_id=1, source_target_pairs={{0,8},{8,16},{16,24},{24,0},{1,9},{9,17},{17,25},{25,1},{2,10},{10... | collective-permute-start | bytes 1572872 | tf_op jit(solution)/shard_map/ppermute | solution.py:30
  104.6 8.6 %collective-permute-start.1 = (f32[1024,128]{0,1:T(8,128)S(1)}, f32[1024,128]{0,1:T(8,128)S(1)}, u32[]{:S(2)}, u32[]{:S(2)}) collective-permute-start(f32[1024,128]{0,1:T(8,128)S(1)} %collective-permute-done), channel_id=1, source_target_pairs={{0,8},{8,16},{16,24},{24,0},{1,9},{9,17},{17,25},{25,1},{2,10},{10... | collective-permute-start | bytes 1572872 | tf_op jit(solution)/shard_map/ppermute | solution.py:30
  113.2 8.6 %collective-permute-start.2 = (f32[1024,128]{0,1:T(8,128)S(1)}, f32[1024,128]{0,1:T(8,128)S(1)}, u32[]{:S(2)}, u32[]{:S(2)}) collective-permute-start(f32[1024,128]{0,1:T(8,128)S(1)} %collective-permute-done.1), channel_id=1, source_target_pairs={{0,8},{8,16},{16,24},{24,0},{1,9},{9,17},{17,25},{25,1},{2,10},{10... | collective-permute-start | bytes 1572872 | tf_op jit(solution)/shard_map/ppermute | solution.py:30
  122.2 3.9 %copy-start.2 = (f32[1024,1024]{0,1:T(8,128)}, f32[1024,1024]{0,1:T(8,128)S(1)}, u32[]{:S(2)}) copy-start(f32[1024,1024]{0,1:T(8,128)S(1)} %constant_dynamic-update-slice_fusion) | copy-start | bytes 12582916
  127.1 54.5 %copy-start.1 = (bf16[2,64,4096]{2,1,0:T(8,128)(2,1)S(1)}, bf16[2,64,4096]{2,1,0:T(8,128)(2,1)}, u32[]{:S(2)}) copy-start(bf16[2,64,4096]{2,1,0:T(8,128)(2,1)} %param.8) | copy-start | bytes 3145732
  181.5 9.1 %copy-start.5 = (f32[1024,128]{1,0:T(8,128)}, f32[1024,128]{1,0:T(8,128)S(1)}, u32[]{:S(2)}) copy-start(f32[1024,128]{1,0:T(8,128)S(1)} %fusion.10) | copy-start | bytes 1572868
  181.7 9.0 %slice-start = ((s8[16777216]{0:T(1024)(128)(4,1)}), s8[4194304]{0:T(1024)(128)(4,1)S(1)}, s32[]{:S(2)}) async-start(s8[16777216]{0:T(1024)(128)(4,1)} %bitcast.73), calls=%async_computation.1 | async-start | bytes 8388608
  182.4 8.2 %copy-start.3 = (bf16[2,128,4096]{2,1,0:T(8,128)(2,1)}, bf16[2,128,4096]{2,1,0:T(8,128)(2,1)S(1)}, u32[]{:S(2)}) copy-start(bf16[2,128,4096]{2,1,0:T(8,128)(2,1)S(1)} %convolution_convert_fusion) | copy-start | bytes 6291460
  182.4 8.2 %slice-start.1 = ((s8[16777216]{0:T(1024)(128)(4,1)}), s8[4194304]{0:T(1024)(128)(4,1)S(1)}, s32[]{:S(2)}) async-start(s8[16777216]{0:T(1024)(128)(4,1)} %bitcast.73), calls=%async_computation.2 | async-start | bytes 8388608
  182.4 8.2 %slice-start.2 = ((s8[16777216]{0:T(1024)(128)(4,1)}), s8[4194304]{0:T(1024)(128)(4,1)S(1)}, s32[]{:S(2)}) async-start(s8[16777216]{0:T(1024)(128)(4,1)} %bitcast.73), calls=%async_computation.3 | async-start | bytes 8388608
  182.5 8.3 %slice-start.3 = ((s8[16777216]{0:T(1024)(128)(4,1)}), s8[4194304]{0:T(1024)(128)(4,1)S(1)}, s32[]{:S(2)}) async-start(s8[16777216]{0:T(1024)(128)(4,1)} %bitcast.73), calls=%async_computation.4 | async-start | bytes 8388608
Sparse Core Ops, SparseCore 0:
  20.3 75.4 all-reduce.1
